TPU v7x, 256 devices: a whole 4x4x8 slice. The times are simulated.
256 devices in a mesh: dp: 8 (over y, core), space: 32 (over z, x).
Axes of the slice: x: 4, y: 4, z: 8, core: 2. Of those that a mesh axis runs over, the one named last changes fastest.
Arguments:
- features: bfloat16 [8, 64, 64, 256], P('dp', None, 'space'), may hold values from -6 to 6
- kernel_a: bfloat16 [27, 64, 128], replicated, may hold values from -0.15625 to 0.15625
- kernel_b: bfloat16 [27, 128, 256], replicated, may hold values from -0.109375 to 0.109375
- upstream: bfloat16 [8, 256, 32, 64], P('dp', None, 'space'), may hold values from -24 to 24
Outputs:
- grad_input: bfloat16 [8, 64, 64, 256], P('dp', None, 'space')
- grad_kernel_a: float32 [27, 64, 128], replicated
- grad_kernel_b: float32 [27, 128, 256], P(None, None, 'space')
All inputs are finite; a program needn't handle non-finite values.
Results may differ from a plain program's by a relative error of at most 0.0075.
Values may be sent and summed in bfloat16 or wider, within the bound.
A program may use at most 64 MiB of HBM per device.

v0:
```python
import math
import jax
import jax.numpy as jnp
from jax import lax
from jax.sharding import PartitionSpec as P

GY = 16
GZ = 16


def with_halo(value, sides, width):
    for axis, dim in sides:
        count, length = (lax.axis_size(axis), value.shape[dim])
        up = [(i, (i + 1) % count) for i in range(count - 1)]
        down = [(j, i) for i, j in up]
        last = lax.slice_in_dim(value, length - width, length, axis=dim)
        leading = lax.slice_in_dim(value, 0, width, axis=dim)
        before = lax.ppermute(last, axis, up)
        after = lax.ppermute(leading, axis, down)
        value = jnp.concatenate([before, value, after], axis=dim)
    return value


def tap_view(padded_flat, off_x, off_y, off_z, planes, span_z, cell_count, column):
    shift_z = off_z - 1
    keep_mask = ((column + shift_z >= 0) & (column + shift_z < span_z)).astype(padded_flat.dtype)
    begin = off_y * span_z + off_z
    return padded_flat[:, :, off_x : off_x + planes, begin : begin + cell_count] * keep_mask


def pad_cells(source, span_z):
    return jnp.pad(source, ((0, 0), (0, 0), (0, 0), (span_z + 1, span_z + 1)))


def pad_planes(source):
    return jnp.pad(source, ((0, 0), (0, 0), (1, 1), (0, 0)))


def conv_forward(rimmed, kernel, planes, span_y, span_z):
    cell_count = span_y * span_z
    padded_flat = pad_cells(rimmed, span_z)
    column = lax.broadcasted_iota(jnp.int32, (cell_count,), 0) % span_z
    summed = None
    for tap_index in range(27):
        shifted = tap_view(
            padded_flat,
            tap_index // 9,
            tap_index // 3 % 3,
            tap_index % 3,
            planes,
            span_z,
            cell_count,
            column,
        )
        product = jnp.einsum(
            "io,sixn->soxn", kernel[tap_index], shifted, preferred_element_type=jnp.float32
        )
        summed = product if summed is None else summed + product
    return summed


def conv_transposed(rimmed, kernel, planes, span_y, span_z):
    cell_count = span_y * span_z
    padded_flat = pad_cells(rimmed, span_z)
    column = lax.broadcasted_iota(jnp.int32, (cell_count,), 0) % span_z
    summed = None
    for tap_index in range(27):
        shifted = tap_view(
            padded_flat,
            2 - tap_index // 9,
            2 - tap_index // 3 % 3,
            2 - tap_index % 3,
            planes,
            span_z,
            cell_count,
            column,
        )
        product = jnp.einsum(
            "io,soxn->sixn", kernel[tap_index], shifted, preferred_element_type=jnp.float32
        )
        summed = product if summed is None else summed + product
    return summed


def kernel_grad(rimmed, gradient, planes, span_y, span_z):
    cell_count = span_y * span_z
    padded_flat = pad_cells(rimmed, span_z)
    column = lax.broadcasted_iota(jnp.int32, (cell_count,), 0) % span_z
    terms = []
    for tap_index in range(27):
        shifted = tap_view(
            padded_flat,
            tap_index // 9,
            tap_index // 3 % 3,
            tap_index % 3,
            planes,
            span_z,
            cell_count,
            column,
        )
        terms.append(
            jnp.einsum("sixn,soxn->io", shifted, gradient, preferred_element_type=jnp.float32)
        )
    return jnp.stack(terms)


def silu_slope(value):
    sigma = jax.nn.sigmoid(value)
    return sigma * (1.0 + value * (1.0 - sigma))


def body(features, kernel_a, kernel_b, upstream):
    samples = features.shape[0]
    planes = features.shape[2]
    half_planes = planes // 2
    half_y, half_z = (GY // 2, GZ // 2)
    rimmed_in = with_halo(features, (("space", 2),), 1)
    pre_a = conv_forward(rimmed_in, kernel_a, planes, GY, GZ)
    filters_a = pre_a.shape[1]
    pooled = (
        jax.nn.silu(pre_a)
        .reshape(samples, filters_a, half_planes, 2, half_y, 2, half_z, 2)
        .mean(axis=(3, 5, 7))
    )
    pooled = pooled.reshape(samples, filters_a, half_planes, half_y * half_z).astype(jnp.bfloat16)
    per_device = kernel_b.shape[2] // lax.axis_size("space")
    gathered = lax.all_gather(pooled, "space", axis=2, tiled=True)
    full_planes = gathered.shape[2]
    own_kernel = lax.dynamic_slice_in_dim(
        kernel_b, lax.axis_index("space") * per_device, per_device, 2
    )
    padded_pooled = pad_planes(gathered)
    pre_b = conv_forward(padded_pooled, own_kernel, full_planes, half_y, half_z)
    upstream_own = lax.all_to_all(upstream, "space", split_axis=1, concat_axis=2, tiled=True)
    grad_pre_b = (upstream_own.astype(jnp.float32) * silu_slope(pre_b)).astype(jnp.bfloat16)
    part_b = kernel_grad(padded_pooled, grad_pre_b, full_planes, half_y, half_z)
    padded_grad = pad_planes(grad_pre_b)
    term_rows = conv_transposed(
        padded_grad, own_kernel, half_planes * lax.axis_size("space"), half_y, half_z
    )
    own_rows = lax.psum_scatter(
        jnp.transpose(term_rows, (2, 0, 1, 3)), "space", scatter_dimension=0, tiled=True
    )
    grad_pool = jnp.transpose(own_rows, (1, 2, 0, 3))
    samples_all = samples * lax.axis_size("dp")
    cells_all = planes * lax.axis_size("space") * GY * GZ
    scale_a = 1.0 / math.sqrt(samples_all * cells_all)
    scale_b = 1.0 / math.sqrt(samples_all * cells_all / 8)
    grad_kernel_b = lax.psum(part_b, "dp") * scale_b
    spread = jnp.broadcast_to(
        grad_pool.reshape(samples, filters_a, half_planes, 1, half_y, 1, half_z, 1),
        (samples, filters_a, half_planes, 2, half_y, 2, half_z, 2),
    )
    spread = spread.reshape(samples, filters_a, planes, GY * GZ)
    grad_pre_a = (spread * 0.125 * silu_slope(pre_a)).astype(jnp.bfloat16)
    part_a = kernel_grad(rimmed_in, grad_pre_a, planes, GY, GZ)
    grad_kernel_a = lax.psum(part_a, ("dp", "space")) * scale_a
    rimmed_back = with_halo(grad_pre_a, (("space", 2),), 1)
    grad_input = conv_transposed(rimmed_back, kernel_a, planes, GY, GZ).astype(jnp.bfloat16)
    return (grad_input, grad_kernel_a, grad_kernel_b)


def solution(mesh):
    return jax.shard_map(
        body,
        mesh=mesh,
        in_specs=(P("dp", None, "space", None), P(), P(), P("dp", None, "space", None)),
        out_specs=(P("dp", None, "space", None), P(), P(None, None, "space")),
        check_vma=False,
    )
```

profile of v0, /device:TPU:1, one launch (start us, length us, event | category | flops | bytes accessed | tf_op | source)
XLA Modules:
  0.0 672.9 jit_solution(3354463360023690337)
XLA Ops:
  9.1 3.9 collective-permute-start
  17.5 12.8 %all-to-all-start = ((bf16[32,2,256]{2,1,0:T(2,128)(2,1)}), bf16[32,2,256]{2,1,0:T(2,128)(2,1)S(1)}, u32[]{:S(2)}, u32[]{:S(2)}) async-start(bf16[32,2,256]{2,1,0:T(2,128)(2,1)} %reshape.962), calls=%async_computation | async-start | bytes 65536 | tf_op jit(solution)/shard_map/all_to_all | solution.py:134
  30.5 1.5 select_maximum_fusion
  33.1 1.5 fusion.371
  42.4 38.8 %all_gather.3 = bf16[1,128,32,64]{1,3,0,2:T(8,128)(2,1)S(1)} all-gather(bf16[1,128,1,64]{1,3,0,2:T(8,128)(2,1)S(1)} %fusion.606), channel_id=1, replica_groups=mesh['dp'=8,'space'=32] {'space'}, dimensions={2}, use_global_device_ids=true | all-gather | bytes 540672 | tf_op jit(solution)/shard_map/all_gather | solution.py:127
  102.7 1.9 multiply_convert_fusion.1
  105.6 1.7 fusion.440
  107.9 1.7 convolution_bitcast_fusion.2
  109.6 1.6 convolution_bitcast_fusion.5
  111.2 1.6 convolution_bitcast_fusion.7
  112.9 1.6 convolution_bitcast_fusion.8
  114.5 1.7 convolution_bitcast_fusion.3
  116.2 1.9 convolution_bitcast_fusion.6
  118.1 1.6 convolution_bitcast_fusion.9
  119.7 1.7 convolution_bitcast_fusion
  145.9 1.9 convolution_add_fusion.14
  157.9 2.1 fusion.12
  160.0 60.2 %all-reduce.11.cloned.1.call-done = f32[27,128,8]{1,2,0:T(8,128)} async-done(((f32[27,128,8]{1,2,0:T(8,128)}), f32[27,128,8]{1,2,0:T(8,128)}) %all-reduce.11.cloned.1.call-update) | async-done | bytes 110608 | tf_op jit(solution)/shard_map/psum | solution.py:149
  220.2 1.6 broadcast_multiply_fusion.1
  221.8 161.0 %reduce-scatter.2.cloned.1.call-done = f32[1,1,128,64]{2,3,0,1:T(8,128)} async-done(((f32[32,1,128,64]{2,3,0,1:T(8,128)}), f32[1,1,128,64]{2,3,0,1:T(8,128)}) %reduce-scatter.2.cloned.1.call-update) | async-done | bytes 32784 | tf_op jit(solution)/shard_map/reduce_scatter | solution.py:141
  393.9 2.2 collective-permute-start.2
  398.5 2.8 collective-permute-done.3
  408.7 254.2 %all-reduce.9.cloned.1.call-done = f32[27,64,128]{2,1,0:T(8,128)} async-done(((f32[27,64,128]{2,1,0:T(8,128)}), f32[27,64,128]{2,1,0:T(8,128)}) %all-reduce.9.cloned.1.call-update) | async-done | bytes 884752 | tf_op jit(solution)/shard_map/psum | solution.py:157
  662.9 2.2 broadcast_multiply_fusion
  (323 shorter events, 91.8 us)
Async XLA Ops:
  8.0 73.2 %copy-start = (bf16[27,128,256]{2,1,0:T(8,128)(2,1)S(1)}, bf16[27,128,256]{2,1,0:T(8,128)(2,1)}, u32[]{:S(2)}) copy-start(bf16[27,128,256]{2,1,0:T(8,128)(2,1)} %param.6) | copy-start | bytes 5308420
  9.1 21.3 %collective-permute-start = (bf16[1,64,1,256]{3,2,1,0:T(2,128)(2,1)S(1)}, bf16[1,64,1,256]{3,2,1,0:T(2,128)(2,1)S(1)}, u32[]{:S(2)}, u32[]{:S(2)}) collective-permute-start(bf16[1,64,1,256]{3,2,1,0:T(2,128)(2,1)S(1)} %get-tuple-element.50), channel_id=1, source_target_pairs={{0,1},{1,2},{2,3},{3,4},{4,5},{5,6},{6,7},{7,8},{8,9},{9,10},{10,1... | collective-permute-start | bytes 98312 | tf_op jit(solution)/shard_map/ppermute | solution.py:18
  13.1 17.4 %collective-permute-start.1 = (bf16[1,64,1,256]{3,2,1,0:T(2,128)(2,1)S(1)}, bf16[1,64,1,256]{3,2,1,0:T(2,128)(2,1)S(1)}, u32[]{:S(2)}, u32[]{:S(2)}) collective-permute-start(bf16[1,64,1,256]{3,2,1,0:T(2,128)(2,1)S(1)} %get-tuple-element.51), channel_id=1, source_target_pairs={{1,0},{2,1},{3,2},{4,3},{5,4},{6,5},{7,6},{8,7},{9,8},{10,9},{11,1... | collective-permute-start | bytes 98312 | tf_op jit(solution)/shard_map/ppermute | solution.py:19
  17.5 84.9 %all-to-all-start = ((bf16[32,2,256]{2,1,0:T(2,128)(2,1)}), bf16[32,2,256]{2,1,0:T(2,128)(2,1)S(1)}, u32[]{:S(2)}, u32[]{:S(2)}) async-start(bf16[32,2,256]{2,1,0:T(2,128)(2,1)} %reshape.962), calls=%async_computation | async-start | bytes 65536 | tf_op jit(solution)/shard_map/all_to_all | solution.py:134
  30.3 189.9 %all-reduce.11.cloned.1.call-start = ((), (), s32[]{:S(2)}) async-start(), calls=%async_computation.4 | async-start | bytes 221184 | tf_op jit(solution)/shard_map/psum | solution.py:149
  81.2 23.5 %copy-start.10 = (bf16[1,128,34,64]{1,3,0,2:T(8,128)(2,1)}, bf16[1,128,34,64]{1,3,0,2:T(8,128)(2,1)S(1)}, u32[]{:S(2)}) copy-start(bf16[1,128,34,64]{1,3,0,2:T(8,128)(2,1)S(1)} %pad.27) | copy-start | bytes 1671172
  145.8 236.9 %reduce-scatter.2.cloned.1.call-start = ((), (), s32[]{:S(2)}) async-start(), calls=%async_computation.2 | async-start | bytes 1081344 | tf_op jit(solution)/shard_map/reduce_scatter | solution.py:141
  157.9 225.7 %copy-start.12 = (f32[1,128,2,256]{1,3,2,0:T(8,128)S(1)}, f32[1,128,2,256]{1,3,2,0:T(8,128)}, u32[]{:S(2)}) copy-start(f32[1,128,2,256]{1,3,2,0:T(8,128)} %get-tuple-element.53) | copy-start | bytes 786436
  159.9 226.4 %copy-start.34 = (bf16[64,2,256]{2,1,0:T(2,128)(2,1)S(1)}, bf16[64,2,256]{2,1,0:T(2,128)(2,1)}, u32[]{:S(2)}) copy-start(bf16[64,2,256]{2,1,0:T(2,128)(2,1)} %copy-done.33) | copy-start | bytes 196612
  159.9 228.7 %copy-start.28 = (bf16[64,2,256]{2,1,0:T(2,128)(2,1)S(1)}, bf16[64,2,256]{2,1,0:T(2,128)(2,1)}, u32[]{:S(2)}) copy-start(bf16[64,2,256]{2,1,0:T(2,128)(2,1)} %copy-done.27) | copy-start | bytes 196612
  160.0 230.9 %copy-start.24 = (bf16[64,2,256]{2,1,0:T(2,128)(2,1)S(1)}, bf16[64,2,256]{2,1,0:T(2,128)(2,1)}, u32[]{:S(2)}) copy-start(bf16[64,2,256]{2,1,0:T(2,128)(2,1)} %copy-done.23) | copy-start | bytes 196612
  160.0 231.1 %copy-start.32 = (bf16[64,2,256]{2,1,0:T(2,128)(2,1)S(1)}, bf16[64,2,256]{2,1,0:T(2,128)(2,1)}, u32[]{:S(2)}) copy-start(bf16[64,2,256]{2,1,0:T(2,128)(2,1)} %copy-done.31) | copy-start | bytes 196612
  160.0 231.2 %copy-start.30 = (bf16[64,2,256]{2,1,0:T(2,128)(2,1)S(1)}, bf16[64,2,256]{2,1,0:T(2,128)(2,1)}, u32[]{:S(2)}) copy-start(bf16[64,2,256]{2,1,0:T(2,128)(2,1)} %copy-done.29) | copy-start | bytes 196612
  160.0 502.9 %all-reduce.9.cloned.1.call-start = ((), (), s32[]{:S(2)}) async-start(), calls=%async_computation.3 | async-start | bytes 1769472 | tf_op jit(solution)/shard_map/psum | solution.py:157
  221.8 169.6 %copy-start.18 = (bf16[64,2,256]{2,1,0:T(2,128)(2,1)S(1)}, bf16[64,2,256]{2,1,0:T(2,128)(2,1)}, u32[]{:S(2)}) copy-start(bf16[64,2,256]{2,1,0:T(2,128)(2,1)} %copy-done.17) | copy-start | bytes 196612
  383.5 8.0 %copy-start.26 = (bf16[64,2,256]{2,1,0:T(2,128)(2,1)S(1)}, bf16[64,2,256]{2,1,0:T(2,128)(2,1)}, u32[]{:S(2)}) copy-start(bf16[64,2,256]{2,1,0:T(2,128)(2,1)} %copy-done.25) | copy-start | bytes 196612
  383.6 8.2 %copy-start.58 = (bf16[64,2,256]{2,1,0:T(2,128)(2,1)S(1)}, bf16[64,2,256]{2,1,0:T(2,128)(2,1)}, u32[]{:S(2)}) copy-start(bf16[64,2,256]{2,1,0:T(2,128)(2,1)} %copy-done.57) | copy-start | bytes 196612
  384.7 7.4 %copy-start.22 = (bf16[64,2,256]{2,1,0:T(2,128)(2,1)S(1)}, bf16[64,2,256]{2,1,0:T(2,128)(2,1)}, u32[]{:S(2)}) copy-start(bf16[64,2,256]{2,1,0:T(2,128)(2,1)} %copy-done.21) | copy-start | bytes 196612
  392.5 8.8 %copy-start.16 = (bf16[27,64,128]{2,1,0:T(8,128)(2,1)S(1)}, bf16[27,64,128]{2,1,0:T(8,128)(2,1)}, u32[]{:S(2)}) copy-start(bf16[27,64,128]{2,1,0:T(8,128)(2,1)} %param.5) | copy-start | bytes 1327108
  392.5 8.8 %copy-start.68 = (bf16[256]{0:T(256)(128)(2,1)S(1)}, bf16[256]{0:T(256)(128)(2,1)}, u32[]{:S(2)}) copy-start(bf16[256]{0:T(256)(128)(2,1)} %copy-done.67) | copy-start | bytes 1540
  393.2 8.7 %copy-start.64 = (bf16[256]{0:T(256)(128)(2,1)S(1)}, bf16[256]{0:T(256)(128)(2,1)}, u32[]{:S(2)}) copy-start(bf16[256]{0:T(256)(128)(2,1)} %copy-done.63) | copy-start | bytes 1540
  393.7 8.6 %copy-start.66 = (bf16[256]{0:T(256)(128)(2,1)S(1)}, bf16[256]{0:T(256)(128)(2,1)}, u32[]{:S(2)}) copy-start(bf16[256]{0:T(256)(128)(2,1)} %copy-done.65) | copy-start | bytes 1540
  393.9 4.6 collective-permute-start.2
  396.1 5.2 collective-permute-start.3
  (53 other events, 201.4 us)
Sparse Core Ops, SparseCore 0:
  146.0 74.2 all-reduce.10
Sparse Core Ops, SparseCore 1:
  160.0 222.6 reduce-scatter.1
  398.6 264.3 all-reduce.8
where the time goes:
time: 680 us; the launch traced here: 673 us
  waiting for transfers between devices  478 us (70%)
  matrix products  99.3 us (15%)
  blocking collectives  38.8 us (6%)
  starting transfers between devices  21.6 us (3%)
  between operations  17.5 us (3%)
  other arithmetic  10.4 us (2%)
  local copies, waits for them, and re-layouts  7.13 us (1%)
    psum x1, waiting for transfers between devices, body(): grad_kernel_a = lax.psum(part_a, ('dp', 'space')) * scale_a  254 us
    reduce_scatter x1, waiting for transfers between devices, body(): lax.psum_scatter(jnp.transpose(term_rows, (2, 0, 1, 3)), 'space', scatter...  161 us
    psum x1, waiting for transfers between devices, body(): grad_kernel_b = lax.psum(part_b, 'dp') * scale_b  60.2 us
    all_gather x1, blocking collectives, body(): gathered = lax.all_gather(pooled, 'space', axis=2, tiled=True)  38.8 us
    dot_general x54, matrix products, conv_transposed(): jnp.einsum('io,soxn->sixn', kernel[tap_index], shifted, preferred_element...  36.3 us
    dot_general x54, matrix products, kernel_grad(): jnp.einsum('sixn,soxn->io', shifted, gradient, preferred_element_type=jnp...  33.3 us
    dot_general x54, matrix products, conv_forward(): jnp.einsum('io,sixn->soxn', kernel[tap_index], shifted, preferred_element...  29.7 us
  transfers between devices with their start and end apart: 8, of which 4 were waited for; matrix products, arithmetic and copies ran while one was open for 8% of the time, Pallas kernels for 0%

commit v1 on v0

--- a/solution.py
+++ b/solution.py
@@ -1,3 +1,4 @@
+import functools
 import math
 import jax
 import jax.numpy as jnp
@@ -6,6 +7,18 @@
 
 GY = 16
 GZ = 16
+
+
+def _end_levels_all(sample, row_axis):
+    return jnp.concatenate(
+        jax.lax.all_to_all(
+            jnp.stack(tuple((sample for _ in range(jax.lax.axis_size(row_axis))))), row_axis, 0, 0
+        ),
+        axis=2,
+    )
+
+
+name_series = functools.partial(_end_levels_all, row_axis="space")
 
 
 def with_halo(value, sides, width):
@@ -124,7 +137,7 @@
     )
     pooled = pooled.reshape(samples, filters_a, half_planes, half_y * half_z).astype(jnp.bfloat16)
     per_device = kernel_b.shape[2] // lax.axis_size("space")
-    gathered = lax.all_gather(pooled, "space", axis=2, tiled=True)
+    gathered = name_series(pooled)
     full_planes = gathered.shape[2]
     own_kernel = lax.dynamic_slice_in_dim(
         kernel_b, lax.axis_index("space") * per_device, per_device, 2

time: 680 us -> 647 us (0.951)
  blocking collectives: 38.8 us -> 0 us
  starting transfers between devices: 21.6 us -> 31.6 us
    all_gather x1 -> x0, blocking collectives: 38.8 us -> none  [body(): gathered = lax.all_gather(pooled, 'space', axis=2, tiled=True)]
    all_to_all x0 -> x1, waiting for transfers between devices: none -> 14.2 us  [_end_levels_all(): jax.lax.all_to_all(jnp.stack(tuple((sample for _ in range(jax.lax.axis_si...]
    psum x1, waiting for transfers between devices: 60.2 us -> 48.3 us  [body(): grad_kernel_b = lax.psum(part_b, 'dp') * scale_b]
    all_to_all x0 -> x1, starting transfers between devices: none -> 9.22 us  [_end_levels_all(): jax.lax.all_to_all(jnp.stack(tuple((sample for _ in range(jax.lax.axis_si...]
  transfers between devices with their start and end apart: 8 -> 9, of which waited for: 4 -> 5; matrix products, arithmetic and copies ran while one was open for 8% -> 6% of each run, Pallas kernels for 0% -> 0%
where the time goes in v1:
time: 647 us; the launch traced here: 640 us
  waiting for transfers between devices  480 us (74%)
  matrix products  92.7 us (14%)
  starting transfers between devices  31.6 us (5%)
  between operations  17.4 us (3%)
  other arithmetic  10.4 us (2%)
  local copies, waits for them, and re-layouts  8.05 us (1%)
    psum x1, waiting for transfers between devices, body(): grad_kernel_a = lax.psum(part_a, ('dp', 'space')) * scale_a  254 us
    reduce_scatter x1, waiting for transfers between devices, body(): lax.psum_scatter(jnp.transpose(term_rows, (2, 0, 1, 3)), 'space', scatter...  161 us
    psum x1, waiting for transfers between devices, body(): grad_kernel_b = lax.psum(part_b, 'dp') * scale_b  48.3 us
    dot_general x54, matrix products, conv_transposed(): jnp.einsum('io,soxn->sixn', kernel[tap_index], shifted, preferred_element...  36.3 us
    dot_general x54, matrix products, kernel_grad(): jnp.einsum('sixn,soxn->io', shifted, gradient, preferred_element_type=jnp...  33.2 us
    dot_general x54, matrix products, conv_forward(): jnp.einsum('io,sixn->soxn', kernel[tap_index], shifted, preferred_element...  23.2 us
    all_to_all x1, waiting for transfers between devices, _end_levels_all(): jax.lax.all_to_all(jnp.stack(tuple((sample for _ in range(jax.lax.axis_si...  14.2 us
  transfers between devices with their start and end apart: 9, of which 5 were waited for; matrix products, arithmetic and copies ran while one was open for 6% of the time, Pallas kernels for 0%

profile of v1, /device:TPU:1, one launch (start us, length us, event | category | flops | bytes accessed | tf_op | source)
XLA Modules:
  0.0 640.4 jit_solution(14732429816514827848)
XLA Ops:
  9.1 3.9 collective-permute-start
  17.5 12.8 %all-to-all-start = ((bf16[32,2,256]{2,1,0:T(2,128)(2,1)}), bf16[32,2,256]{2,1,0:T(2,128)(2,1)S(1)}, u32[]{:S(2)}, u32[]{:S(2)}) async-start(bf16[32,2,256]{2,1,0:T(2,128)(2,1)} %reshape.972), calls=%async_computation | async-start | bytes 65536 | tf_op jit(solution)/shard_map/all_to_all | solution.py:147
  30.4 1.5 select_maximum_fusion
  33.0 1.5 fusion.368
  43.2 9.2 %all-to-all-start.1 = ((bf16[32,1,128,1,64]{2,4,3,1,0:T(8,128)(2,1)}), bf16[32,1,128,1,64]{2,4,3,1,0:T(8,128)(2,1)S(1)}, u32[]{:S(2)}, u32[]{:S(2)}) async-start(bf16[32,1,128,1,64]{2,4,3,1,0:T(8,128)(2,1)} %stack.203), calls=%async_computation.1 | async-start | bytes 1048576 | tf_op jit(solution)/shard_map/all_to_all | solution.py:14
  53.2 14.2 %all-to-all-done.1 = bf16[32,1,128,1,64]{2,4,3,1,0:T(8,128)(2,1)S(1)} async-done(((bf16[32,1,128,1,64]{2,4,3,1,0:T(8,128)(2,1)}), bf16[32,1,128,1,64]{2,4,3,1,0:T(8,128)(2,1)S(1)}, u32[]{:S(2)}, u32[]{:S(2)}) %all-to-all-start.1) | async-done | bytes 524320 | tf_op jit(solution)/shard_map/all_to_all | solution.py:14
  85.0 1.7 fusion.437
  87.4 1.7 convolution_bitcast_fusion.2
  89.0 1.6 convolution_bitcast_fusion.5
  90.7 1.6 convolution_bitcast_fusion.7
  92.3 1.6 convolution_bitcast_fusion.8
  93.9 1.7 convolution_bitcast_fusion.3
  95.6 1.7 convolution_bitcast_fusion.6
  97.3 1.6 convolution_bitcast_fusion.9
  98.9 1.9 convolution_bitcast_fusion
  125.3 1.9 convolution_add_fusion.14
  137.2 2.1 fusion.12
  139.6 48.3 %all-reduce.11.cloned.1.call-done = f32[27,128,8]{1,2,0:T(8,128)} async-done(((f32[27,128,8]{1,2,0:T(8,128)}), f32[27,128,8]{1,2,0:T(8,128)}) %all-reduce.11.cloned.1.call-update) | async-done | bytes 110608 | tf_op jit(solution)/shard_map/psum | solution.py:162
  188.0 1.6 broadcast_multiply_fusion.1
  189.5 160.8 %reduce-scatter.2.cloned.1.call-done = f32[1,1,128,64]{2,3,0,1:T(8,128)} async-done(((f32[32,1,128,64]{2,3,0,1:T(8,128)}), f32[1,1,128,64]{2,3,0,1:T(8,128)}) %reduce-scatter.2.cloned.1.call-update) | async-done | bytes 32784 | tf_op jit(solution)/shard_map/reduce_scatter | solution.py:154
  361.5 2.3 collective-permute-start.2
  366.2 2.8 collective-permute-done.3
  376.4 254.1 %all-reduce.9.cloned.1.call-done = f32[27,64,128]{2,1,0:T(8,128)} async-done(((f32[27,64,128]{2,1,0:T(8,128)}), f32[27,64,128]{2,1,0:T(8,128)}) %all-reduce.9.cloned.1.call-update) | async-done | bytes 884752 | tf_op jit(solution)/shard_map/psum | solution.py:170
  630.5 2.2 broadcast_multiply_fusion
  (321 shorter events, 88.8 us)
Async XLA Ops:
  8.0 59.5 %copy-start = (bf16[27,128,256]{2,1,0:T(8,128)(2,1)S(1)}, bf16[27,128,256]{2,1,0:T(8,128)(2,1)}, u32[]{:S(2)}) copy-start(bf16[27,128,256]{2,1,0:T(8,128)(2,1)} %param.6) | copy-start | bytes 5308420
  9.1 21.3 %collective-permute-start = (bf16[1,64,1,256]{3,2,1,0:T(2,128)(2,1)S(1)}, bf16[1,64,1,256]{3,2,1,0:T(2,128)(2,1)S(1)}, u32[]{:S(2)}, u32[]{:S(2)}) collective-permute-start(bf16[1,64,1,256]{3,2,1,0:T(2,128)(2,1)S(1)} %get-tuple-element.50), channel_id=1, source_target_pairs={{0,1},{1,2},{2,3},{3,4},{4,5},{5,6},{6,7},{7,8},{8,9},{9,10},{10,1... | collective-permute-start | bytes 98312 | tf_op jit(solution)/shard_map/ppermute | solution.py:31
  13.1 17.3 %collective-permute-start.1 = (bf16[1,64,1,256]{3,2,1,0:T(2,128)(2,1)S(1)}, bf16[1,64,1,256]{3,2,1,0:T(2,128)(2,1)S(1)}, u32[]{:S(2)}, u32[]{:S(2)}) collective-permute-start(bf16[1,64,1,256]{3,2,1,0:T(2,128)(2,1)S(1)} %get-tuple-element.51), channel_id=1, source_target_pairs={{1,0},{2,1},{3,2},{4,3},{5,4},{6,5},{7,6},{8,7},{9,8},{10,9},{11,1... | collective-permute-start | bytes 98312 | tf_op jit(solution)/shard_map/ppermute | solution.py:32
  17.5 24.7 %all-to-all-start = ((bf16[32,2,256]{2,1,0:T(2,128)(2,1)}), bf16[32,2,256]{2,1,0:T(2,128)(2,1)S(1)}, u32[]{:S(2)}, u32[]{:S(2)}) async-start(bf16[32,2,256]{2,1,0:T(2,128)(2,1)} %reshape.972), calls=%async_computation | async-start | bytes 65536 | tf_op jit(solution)/shard_map/all_to_all | solution.py:147
  43.2 24.2 %all-to-all-start.1 = ((bf16[32,1,128,1,64]{2,4,3,1,0:T(8,128)(2,1)}), bf16[32,1,128,1,64]{2,4,3,1,0:T(8,128)(2,1)S(1)}, u32[]{:S(2)}, u32[]{:S(2)}) async-start(bf16[32,1,128,1,64]{2,4,3,1,0:T(8,128)(2,1)} %stack.203), calls=%async_computation.1 | async-start | bytes 1048576 | tf_op jit(solution)/shard_map/all_to_all | solution.py:14
  52.4 135.6 %all-reduce.11.cloned.1.call-start = ((), (), s32[]{:S(2)}) async-start(), calls=%async_computation.5 | async-start | bytes 221184 | tf_op jit(solution)/shard_map/psum | solution.py:162
  125.2 225.1 %reduce-scatter.2.cloned.1.call-start = ((), (), s32[]{:S(2)}) async-start(), calls=%async_computation.3 | async-start | bytes 1081344 | tf_op jit(solution)/shard_map/reduce_scatter | solution.py:154
  137.2 213.9 %copy-start.10 = (f32[1,128,2,256]{1,3,2,0:T(8,128)S(1)}, f32[1,128,2,256]{1,3,2,0:T(8,128)}, u32[]{:S(2)}) copy-start(f32[1,128,2,256]{1,3,2,0:T(8,128)} %get-tuple-element.53) | copy-start | bytes 786436
  139.3 214.7 %copy-start.32 = (bf16[64,2,256]{2,1,0:T(2,128)(2,1)S(1)}, bf16[64,2,256]{2,1,0:T(2,128)(2,1)}, u32[]{:S(2)}) copy-start(bf16[64,2,256]{2,1,0:T(2,128)(2,1)} %copy-done.31) | copy-start | bytes 196612
  139.3 216.9 %copy-start.26 = (bf16[64,2,256]{2,1,0:T(2,128)(2,1)S(1)}, bf16[64,2,256]{2,1,0:T(2,128)(2,1)}, u32[]{:S(2)}) copy-start(bf16[64,2,256]{2,1,0:T(2,128)(2,1)} %copy-done.25) | copy-start | bytes 196612
  139.3 219.1 %copy-start.22 = (bf16[64,2,256]{2,1,0:T(2,128)(2,1)S(1)}, bf16[64,2,256]{2,1,0:T(2,128)(2,1)}, u32[]{:S(2)}) copy-start(bf16[64,2,256]{2,1,0:T(2,128)(2,1)} %copy-done.21) | copy-start | bytes 196612
  139.3 219.3 %copy-start.30 = (bf16[64,2,256]{2,1,0:T(2,128)(2,1)S(1)}, bf16[64,2,256]{2,1,0:T(2,128)(2,1)}, u32[]{:S(2)}) copy-start(bf16[64,2,256]{2,1,0:T(2,128)(2,1)} %copy-done.29) | copy-start | bytes 196612
  139.4 219.4 %copy-start.28 = (bf16[64,2,256]{2,1,0:T(2,128)(2,1)S(1)}, bf16[64,2,256]{2,1,0:T(2,128)(2,1)}, u32[]{:S(2)}) copy-start(bf16[64,2,256]{2,1,0:T(2,128)(2,1)} %copy-done.27) | copy-start | bytes 196612
  139.4 491.1 %all-reduce.9.cloned.1.call-start = ((), (), s32[]{:S(2)}) async-start(), calls=%async_computation.4 | async-start | bytes 1769472 | tf_op jit(solution)/shard_map/psum | solution.py:170
  189.5 169.4 %copy-start.16 = (bf16[64,2,256]{2,1,0:T(2,128)(2,1)S(1)}, bf16[64,2,256]{2,1,0:T(2,128)(2,1)}, u32[]{:S(2)}) copy-start(bf16[64,2,256]{2,1,0:T(2,128)(2,1)} %copy-done.15) | copy-start | bytes 196612
  351.1 8.0 %copy-start.24 = (bf16[64,2,256]{2,1,0:T(2,128)(2,1)S(1)}, bf16[64,2,256]{2,1,0:T(2,128)(2,1)}, u32[]{:S(2)}) copy-start(bf16[64,2,256]{2,1,0:T(2,128)(2,1)} %copy-done.23) | copy-start | bytes 196612
  351.1 8.2 %copy-start.56 = (bf16[64,2,256]{2,1,0:T(2,128)(2,1)S(1)}, bf16[64,2,256]{2,1,0:T(2,128)(2,1)}, u32[]{:S(2)}) copy-start(bf16[64,2,256]{2,1,0:T(2,128)(2,1)} %copy-done.55) | copy-start | bytes 196612
  352.3 7.4 %copy-start.20 = (bf16[64,2,256]{2,1,0:T(2,128)(2,1)S(1)}, bf16[64,2,256]{2,1,0:T(2,128)(2,1)}, u32[]{:S(2)}) copy-start(bf16[64,2,256]{2,1,0:T(2,128)(2,1)} %copy-done.19) | copy-start | bytes 196612
  360.1 8.9 %copy-start.14 = (bf16[27,64,128]{2,1,0:T(8,128)(2,1)S(1)}, bf16[27,64,128]{2,1,0:T(8,128)(2,1)}, u32[]{:S(2)}) copy-start(bf16[27,64,128]{2,1,0:T(8,128)(2,1)} %param.5) | copy-start | bytes 1327108
  360.1 8.9 %copy-start.66 = (bf16[256]{0:T(256)(128)(2,1)S(1)}, bf16[256]{0:T(256)(128)(2,1)}, u32[]{:S(2)}) copy-start(bf16[256]{0:T(256)(128)(2,1)} %copy-done.65) | copy-start | bytes 1540
  360.8 8.7 %copy-start.62 = (bf16[256]{0:T(256)(128)(2,1)S(1)}, bf16[256]{0:T(256)(128)(2,1)}, u32[]{:S(2)}) copy-start(bf16[256]{0:T(256)(128)(2,1)} %copy-done.61) | copy-start | bytes 1540
  361.3 8.7 %copy-start.64 = (bf16[256]{0:T(256)(128)(2,1)S(1)}, bf16[256]{0:T(256)(128)(2,1)}, u32[]{:S(2)}) copy-start(bf16[256]{0:T(256)(128)(2,1)} %copy-done.63) | copy-start | bytes 1540
  361.5 4.7 collective-permute-start.2
  363.7 5.2 collective-permute-start.3
  (52 other events, 195.1 us)
Sparse Core Ops, SparseCore 0:
  125.3 62.5 all-reduce.10
Sparse Core Ops, SparseCore 1:
  139.4 210.8 reduce-scatter.1
  366.2 264.2 all-reduce.8
